TPU v7x, 128 devices: a whole 4x4x4 slice. The times are simulated.
128 devices in a mesh: grp: 4 (over y), col: 32 (over x, z, core).
Axes of the slice: x: 4, y: 4, z: 4, core: 2. Of those that a mesh axis runs over, the one named last changes fastest.
Arguments:
- blocks: bfloat16 [24576, 32, 1024], P(('grp', 'col'))
- i_index: int32 [24576], P(('grp', 'col')), may hold values from 0 to 63
- j_index: int32 [24576], P(('grp', 'col')), may hold values from 0 to 63
- k_index: int32 [24576], P(('grp', 'col')), may hold values from 0 to 15
- block_count: int32 [128], P(('grp', 'col')), may hold values from 24 to 192, as said below
- b_factor: float32 [65536, 256], P(('grp', 'col'))
- c_factor: float32 [16384, 256], P(('grp', 'col'))
Outputs:
- a_update: float32 [8192, 256], P(('grp', 'col'))
- b_update: float32 [65536, 256], P(('grp', 'col'))
Inputs may be any that keep to these rules, and one draw needn't show every extreme that they name: block_count[d] is the number of live slots of device d = 32 * (grp index) + (col index): its slots d * 192 to d * 192 + block_count[d] - 1; every other slot is ignored. Some device has exactly 192 live slots.
All inputs are finite; a program needn't handle non-finite values.
Results may differ from a plain program's by a relative error of at most 0.005.
The roundings to bfloat16 on the way count: a program that leaves them out, or rounds other values in their place, can miss the bound.
Values may be sent and summed in bfloat16 or wider, within the bound.
No kernel may reach another device: no remote copies, remote signals or barrier semaphores. Data moves between devices by JAX's collectives and lax.ppermute only.
A program may use at most 128 MiB of HBM per device.

v0:
```python
import jax
import jax.numpy as jnp
from jax import lax
from jax.sharding import PartitionSpec as P

A_DEV = 2


def solve_rows(gram, right_side):
    factor_low = lax.linalg.cholesky(gram)
    halfway = lax.linalg.triangular_solve(
        factor_low, right_side, left_side=False, lower=True, transpose_a=True
    )
    return lax.linalg.triangular_solve(
        factor_low, halfway, left_side=False, lower=True, transpose_a=False
    )


def mode_term(
    blocks,
    left_rows,
    left_index,
    tail_rows,
    tail_index,
    target_index,
    live_mask,
    targets,
    first_mode,
):
    block_edge = blocks.shape[1]
    rank_width = left_rows.shape[1]
    group_size = 16
    groups = blocks.shape[0] // group_size
    left_table = left_rows.reshape(-1, block_edge, rank_width)
    tail_table = tail_rows.reshape(-1, block_edge, rank_width)
    target_ids = jnp.arange(targets, dtype=jnp.int32)

    def one_step(running, inputs):
        tensor_group, left_idx, tail_idx, target_idx, alive_row = inputs
        left_blk = left_table[left_idx].astype(jnp.float32)
        tail_blk = tail_table[tail_idx].astype(jnp.float32)
        product = (left_blk[:, :, None, :] * tail_blk[:, None, :, :]).astype(jnp.bfloat16)
        if first_mode:
            result = jnp.einsum(
                "bim,bmr->bir",
                tensor_group,
                product.reshape(group_size, block_edge * block_edge, rank_width),
                preferred_element_type=jnp.float32,
            )
        else:
            result = jnp.einsum(
                "bijk,bikr->bjr",
                tensor_group.reshape(group_size, block_edge, block_edge, block_edge),
                product,
                preferred_element_type=jnp.float32,
            )
        select = (target_idx[None, :] == target_ids[:, None]).astype(jnp.float32) * alive_row[
            None, :
        ]
        update = jnp.dot(
            select,
            result.reshape(group_size, block_edge * rank_width),
            precision=lax.Precision.HIGHEST,
        )
        return (running + update, None)

    inputs = (
        blocks.reshape(groups, group_size, block_edge, block_edge * block_edge),
        left_index.reshape(groups, group_size),
        tail_index.reshape(groups, group_size),
        target_index.reshape(groups, group_size),
        live_mask.reshape(groups, group_size),
    )
    start_value = jnp.zeros((targets, block_edge * rank_width), jnp.float32)
    running, _ = lax.scan(one_step, start_value, inputs)
    return running.reshape(targets * block_edge, rank_width)


def on_device(blocks, i_index, j_index, k_index, block_count, b_factor, c_factor):
    highest = lax.Precision.HIGHEST
    block_edge = blocks.shape[1]
    gram_second, gram_third = lax.psum(
        (
            jnp.dot(b_factor.T, b_factor, precision=highest),
            jnp.dot(c_factor.T, c_factor, precision=highest),
        ),
        ("grp", "col"),
    )
    b_range, c_range = (
        lax.all_gather(b_factor.astype(jnp.bfloat16), "grp", axis=0, tiled=True),
        lax.all_gather(c_factor.astype(jnp.bfloat16), "grp", axis=0, tiled=True),
    )
    live_mask = (jnp.arange(blocks.shape[0], dtype=jnp.int32) < block_count[0]).astype(jnp.float32)
    first_targets = A_DEV * lax.axis_size("col")
    second_targets = b_range.shape[0] // block_edge
    partial_value = mode_term(
        blocks, b_range, j_index, c_range, k_index, i_index, live_mask, first_targets, True
    )
    gram_one = gram_second * gram_third
    whole_sum = lax.psum(partial_value, "col")
    a_whole = solve_rows(gram_one, whole_sum)
    gram_first = lax.psum(jnp.dot(a_whole.T, a_whole, precision=highest), "grp")
    col_norm = jnp.sqrt(jnp.diagonal(gram_first) + 1e-06)
    a_range = (a_whole / col_norm[None, :]).astype(jnp.bfloat16)
    own_rows = A_DEV * block_edge
    a_update = lax.dynamic_slice_in_dim(a_whole, lax.axis_index("col") * own_rows, own_rows, 0)
    gram_two = gram_first / (col_norm[:, None] * col_norm[None, :]) * gram_third
    partial_two = mode_term(
        blocks, a_range, i_index, c_range, k_index, j_index, live_mask, second_targets, False
    )
    own_two = lax.psum_scatter(partial_two, "grp", scatter_dimension=0, tiled=True)
    b_update = solve_rows(gram_two, own_two)
    return (a_update, b_update)


def solution(mesh):
    return jax.shard_map(
        on_device,
        mesh=mesh,
        in_specs=(
            P(("grp", "col"), None, None),
            P(("grp", "col")),
            P(("grp", "col")),
            P(("grp", "col")),
            P(("grp", "col")),
            P(("grp", "col"), None),
            P(("grp", "col"), None),
        ),
        out_specs=(P(("grp", "col"), None), P(("grp", "col"), None)),
        check_vma=False,
    )
```

profile of v0, /device:TPU:0, one launch (start us, length us, event | category | flops | bytes accessed | tf_op | source)
XLA Modules:
  0.0 780.1 jit_solution(10742429783290168959)
XLA Ops:
  15.0 13.0 %all_gather.7 = bf16[512,256]{1,0:T(8,128)(2,1)S(1)} all-gather(bf16[128,256]{1,0:T(8,128)(2,1)S(1)} %convert_element_type.56), channel_id=1, replica_groups=mesh['grp'=4,'col'=32] {'grp'}, dimensions={0}, use_global_device_ids=true | all-gather | bytes 327680 | tf_op jit(solution)/shard_map/all_gather | solution.py:91
  28.0 135.6 %all-reduce.10.cloned.1.call-done = (f32[256,256]{0,1:T(8,128)}, f32[256,256]{0,1:T(8,128)}) async-done(((f32[256,256]{0,1:T(8,128)}, f32[256,256]{0,1:T(8,128)}), (f32[256,256]{0,1:T(8,128)}, f32[256,256]{0,1:T(8,128)})) %all-reduce.10.cloned.1.call-update) | async-done | bytes 524304 | tf_op jit(solution)/shard_map/psum | solution.py:82
  164.8 11.7 %custom-call.29 = f32[128,128]{1,0:T(8,128)S(1)} custom-call(f32[128,128]{1,0:T(8,128)S(1)} %slice.101), custom_call_target="Cholesky" | custom-call | tf_op jit(solution)/shard_map/cholesky/custom-call.2 | solution.py:10
  176.6 9.8 %custom-call.30 = f32[1,128,128]{1,2,0:T(8,128)S(1)} custom-call(f32[1,128,128]{2,1,0:T(8,128)S(1)} %get-tuple-element.262), custom_call_target="InvertDiagBlocksLowerTriangular" | custom-call | tf_op jit(solution)/shard_map/cholesky/custom-call.7 | solution.py:10
  187.1 11.7 %custom-call.31 = f32[128,128]{1,0:T(8,128)S(1)} custom-call(f32[128,128]{1,0:T(8,128)S(1)} %convolution_subtract_fusion.5), custom_call_target="Cholesky" | custom-call | tf_op jit(solution)/shard_map/cholesky/custom-call.3 | solution.py:10
  198.9 141.3 %while.26 = (s32[]{:T(128)}, f32[64,8192]{1,0:T(8,128)S(1)}, s32[12,16]{1,0:T(8,128)S(1)}, f32[12,16]{1,0:T(8,128)S(1)}, bf16[12,16,32,1024]{3,2,1,0:T(8,128)(2,...) while((s32[]{:T(128)}, f32[64,8192]{1,0:T(8,128)S(1)}, ...), condition=%wide.region_1.0_spmd.clone, body=%wide.region_0.0_spmd.clone.sunk | while | flops 378802272 | bytes 27796492 | solution.py:75
  201.6 3.9 multiply_convert_fusion.5
  213.3 3.9 multiply_convert_fusion.5
  225.1 3.9 multiply_convert_fusion.5
  236.8 3.9 multiply_convert_fusion.5
  248.6 3.9 multiply_convert_fusion.5
  260.4 3.9 multiply_convert_fusion.5
  272.1 3.9 multiply_convert_fusion.5
  344.0 4.3 while.24
  348.3 19.7 %custom-call.20 = f32[2,128,128]{1,2,0:T(8,128)S(1)} custom-call(f32[2,128,128]{2,1,0:T(8,128)S(1)} %get-tuple-element.116), custom_call_target="InvertDiagBlocksLowerTriangular" | custom-call | tf_op jit(solution)/shard_map/triangular_solve | solution.py:11
  368.0 80.2 %all-reduce.6.cloned.1.call-done = f32[2048,256]{1,0:T(8,128)} async-done(((f32[2048,256]{1,0:T(8,128)}), f32[2048,256]{1,0:T(8,128)}) %all-reduce.6.cloned.1.call-update) | async-done | bytes 2097168 | tf_op jit(solution)/shard_map/psum | solution.py:100
  456.5 4.2 fusion.33
  461.2 40.8 %all-reduce.8.cloned.1.call-done = f32[256,256]{0,1:T(8,128)} async-done(((f32[256,256]{0,1:T(8,128)}), f32[256,256]{0,1:T(8,128)}) %all-reduce.8.cloned.1.call-update) | async-done | bytes 262160 | tf_op jit(solution)/shard_map/psum | solution.py:102
  507.1 195.0 %while.27 = (s32[]{:T(128)}, f32[64,8192]{1,0:T(8,128)S(1)}, s32[12,16]{1,0:T(8,128)}, f32[12,16]{1,0:T(8,128)}, bf16[12,16,32,1024]{3,2,1,0:T(8,128)(2,1)}, /*i...) while((s32[]{:T(128)}, f32[64,8192]{1,0:T(8,128)S(1)}, ...), condition=%wide.region_11.13_spmd.clone, body=%wide.region_10.12_spmd.clone.sunk | while | flops 378802272 | bytes 15213583 | solution.py:75
  508.4 4.4 reshape.345
  515.3 4.0 fusion.116
  524.7 4.4 reshape.345
  531.5 4.0 fusion.116
  540.9 4.4 reshape.345
  547.8 4.0 fusion.116
  557.2 4.4 reshape.345
  564.0 4.0 fusion.116
  573.4 4.4 reshape.345
  580.3 4.0 fusion.116
  589.7 4.4 reshape.345
  596.5 4.0 fusion.116
  605.9 4.4 reshape.345
  612.8 4.0 fusion.116
  622.2 4.4 reshape.345
  629.0 4.0 fusion.116
  638.4 4.4 reshape.345
  645.3 4.0 fusion.116
  654.7 4.4 reshape.345
  661.5 4.0 fusion.116
  670.9 4.4 reshape.345
  677.8 4.0 fusion.116
  687.2 4.4 reshape.345
  694.0 4.0 fusion.116
  706.2 11.7 %custom-call.32 = f32[128,128]{1,0:T(8,128)S(1)} custom-call(f32[128,128]{1,0:T(8,128)S(1)} %slice.104), custom_call_target="Cholesky" | custom-call | tf_op jit(solution)/shard_map/cholesky/custom-call.2 | solution.py:10
  718.0 9.8 %custom-call.33 = f32[1,128,128]{1,2,0:T(8,128)S(1)} custom-call(f32[1,128,128]{2,1,0:T(8,128)S(1)} %get-tuple-element.258), custom_call_target="InvertDiagBlocksLowerTriangular" | custom-call | tf_op jit(solution)/shard_map/cholesky/custom-call.7 | solution.py:10
  728.5 11.7 %custom-call.34 = f32[128,128]{1,0:T(8,128)S(1)} custom-call(f32[128,128]{1,0:T(8,128)S(1)} %convolution_subtract_fusion.4), custom_call_target="Cholesky" | custom-call | tf_op jit(solution)/shard_map/cholesky/custom-call.3 | solution.py:10
  742.9 4.0 while.25
  746.9 19.8 %custom-call.21 = f32[2,128,128]{1,2,0:T(8,128)S(1)} custom-call(f32[2,128,128]{2,1,0:T(8,128)S(1)} %get-tuple-element.124), custom_call_target="InvertDiagBlocksLowerTriangular" | custom-call | tf_op jit(solution)/shard_map/triangular_solve | solution.py:11
  (415 shorter events, 249.8 us)
Async XLA Ops:
  8.0 5.2 copy-start.5
  8.0 6.0 copy-start.8
  8.0 6.0 copy-start.12
  8.0 6.8 copy-start.13
  8.0 6.9 copy-start.14
  8.0 155.5 %all-reduce.10.cloned.1.call-start = ((), (), s32[]{:S(2)}) async-start(), calls=%async_computation.5 | async-start | bytes 1048576 | tf_op jit(solution)/shard_map/psum | solution.py:82
  13.2 185.7 %all-gather.2.cloned.1.call-start = ((), (), s32[]{:S(2)}) async-start(), calls=%async_computation.1 | async-start | bytes 1310720 | tf_op jit(solution)/shard_map/all_gather | solution.py:90
  14.0 434.3 %all-reduce.6.cloned.1.call-start = ((), (), s32[]{:S(2)}) async-start(), calls=%async_computation.2 | async-start | bytes 4194304 | tf_op jit(solution)/shard_map/psum | solution.py:100
  340.2 1.5 copy-start.10
  340.2 1.5 copy-start.11
  341.8 160.2 %all-reduce.8.cloned.1.call-start = ((), (), s32[]{:S(2)}) async-start(), calls=%async_computation.3 | async-start | bytes 524288 | tf_op jit(solution)/shard_map/psum | solution.py:102
  348.3 103.3 %copy-start.7 = (f32[256,256]{1,0:T(8,128)}, f32[256,256]{1,0:T(8,128)S(1)}, u32[]{:S(2)}) copy-start(f32[256,256]{1,0:T(8,128)S(1)} %get-tuple-element.553) | copy-start | bytes 786436
  348.3 103.3 %copy-start.15 = (s32[2,2]{1,0:T(2,128)}, s32[2,2]{1,0:T(2,128)S(1)}, u32[]{:S(2)}) copy-start(s32[2,2]{1,0:T(2,128)S(1)} %get-tuple-element.571) | copy-start | bytes 52
  448.3 2.4 copy-start.6
  453.6 51.0 %copy-start = (f32[2048,128]{1,0:T(8,128)}, f32[2048,128]{1,0:T(8,128)S(1)}, u32[]{:S(2)}) copy-start(f32[2048,128]{1,0:T(8,128)S(1)} %fusion.48) | copy-start | bytes 3145732
  456.5 4.7 copy-start.2
  460.7 306.1 %reduce-scatter.2.cloned.1.call-start = ((), (), s32[]{:S(2)}) async-start(), calls=%async_computation.4 | async-start | bytes 2621440 | tf_op jit(solution)/shard_map/reduce_scatter | solution.py:111
  703.6 1.2 copy-start.1
  703.6 1.5 copy-start.3
  703.6 2.2 copy-start.4
  703.6 2.2 copy-start.9
  706.0 36.9 %copy-start.16 = (s32[2,2]{1,0:T(2,128)S(1)}, s32[2,2]{1,0:T(2,128)}, u32[]{:S(2)}) copy-start(s32[2,2]{1,0:T(2,128)} %copy-done.15) | copy-start | bytes 52
Sparse Core Ops, SparseCore 0:
  13.8 149.6 all-reduce.9
Sparse Core Ops, SparseCore 1:
  15.9 26.6 all-gather.1
  341.9 106.3 all-reduce.5
  460.8 41.2 all-reduce.7
  703.7 30.0 reduce-scatter.1
where the time goes:
time: 792 us; the launch traced here: 780 us
  waiting for transfers between devices  257 us (32%)
  local copies, waits for them, and re-layouts  166 us (21%)
  other arithmetic  162 us (20%)
  matrix products  159 us (20%)
  between operations  19.7 us (2%)
  blocking collectives  13 us (2%)
    psum x1, waiting for transfers between devices, on_device(): lax.psum((jnp.dot(b_factor.T, b_factor, precision=highest), jnp.dot(c_fac...  136 us
    psum x1, waiting for transfers between devices, on_device(): whole_sum = lax.psum(partial_value, 'col')  80.2 us
    another operation x13, other arithmetic, solve_rows(): factor_low = lax.linalg.cholesky(gram)  68.6 us
    dot_general x24, matrix products, one_step(): jnp.dot(select, result.reshape(group_size, block_edge * rank_width), prec...  55 us
    reshape x12, local copies, waits for them, and re-layouts, one_step(): tensor_group.reshape(group_size, block_edge, block_edge, block_edge)  52.3 us
    dot_general x12, matrix products, one_step(): jnp.einsum('bijk,bikr->bjr', tensor_group.reshape(group_size, block_edge,...  48.5 us
    convert_element_type x12, other arithmetic, one_step(): (left_blk[:, :, None, :] * tail_blk[:, None, :, :]).astype(jnp.bfloat16)  46.2 us
    gather x24, local copies, waits for them, and re-layouts, one_step(): left_blk = left_table[left_idx].astype(jnp.float32)  42.9 us
  transfers between devices with their start and end apart: 5, of which 3 were waited for; matrix products, arithmetic and copies ran while one was open for 15% of the time, Pallas kernels for 0%

commit v1 on v0

--- a/solution.py
+++ b/solution.py
@@ -4,6 +4,11 @@
 from jax.sharding import PartitionSpec as P
 
 A_DEV = 2
+
+
+def by_each_axis(x, one, other):
+    partial = lax.psum(x, one)
+    return lax.psum(partial, other)
 
 
 def solve_rows(gram, right_side):
@@ -79,12 +84,13 @@
 def on_device(blocks, i_index, j_index, k_index, block_count, b_factor, c_factor):
     highest = lax.Precision.HIGHEST
     block_edge = blocks.shape[1]
-    gram_second, gram_third = lax.psum(
+    gram_second, gram_third = by_each_axis(
         (
             jnp.dot(b_factor.T, b_factor, precision=highest),
             jnp.dot(c_factor.T, c_factor, precision=highest),
         ),
-        ("grp", "col"),
+        "col",
+        "grp",
     )
     b_range, c_range = (
         lax.all_gather(b_factor.astype(jnp.bfloat16), "grp", axis=0, tiled=True),

time: 792 us -> 757 us (0.956)
  waiting for transfers between devices: 257 us -> 204 us
  other arithmetic: 162 us -> 183 us
    psum x1, waiting for transfers between devices: 136 us -> 44.8 us  [by_each_axis(): return lax.psum(partial, other)]
    psum x1, waiting for transfers between devices: 80.2 us -> 110 us  [on_device(): whole_sum = lax.psum(partial_value, 'col')]
    convert_element_type x24, other arithmetic: 0.97 us -> 10.6 us  [one_step(): tail_blk = tail_table[tail_idx].astype(jnp.float32)]
    convert_element_type x24, other arithmetic: 0.97 us -> 10.5 us  [one_step(): left_blk = left_table[left_idx].astype(jnp.float32)]
  transfers between devices with their start and end apart: 5 -> 5, of which waited for: 3 -> 4; matrix products, arithmetic and copies ran while one was open for 15% -> 9% of each run, Pallas kernels for 0% -> 0%
where the time goes in v1:
time: 757 us; the launch traced here: 748 us
  waiting for transfers between devices  204 us (27%)
  other arithmetic  183 us (24%)
  local copies, waits for them, and re-layouts  169 us (22%)
  matrix products  158 us (21%)
  between operations  17.7 us (2%)
  blocking collectives  12.9 us (2%)
    psum x1, waiting for transfers between devices, on_device(): whole_sum = lax.psum(partial_value, 'col')  110 us
    another operation x13, other arithmetic, solve_rows(): factor_low = lax.linalg.cholesky(gram)  68.6 us
    dot_general x24, matrix products, one_step(): jnp.dot(select, result.reshape(group_size, block_edge * rank_width), prec...  54.9 us
    reshape x12, local copies, waits for them, and re-layouts, one_step(): tensor_group.reshape(group_size, block_edge, block_edge, block_edge)  52.4 us
    dot_general x12, matrix products, one_step(): jnp.einsum('bijk,bikr->bjr', tensor_group.reshape(group_size, block_edge,...  51.2 us
    convert_element_type x12, other arithmetic, one_step(): (left_blk[:, :, None, :] * tail_blk[:, None, :, :]).astype(jnp.bfloat16)  46.2 us
    psum x1, waiting for transfers between devices, by_each_axis(): return lax.psum(partial, other)  44.8 us
    gather x24, local copies, waits for them, and re-layouts, one_step(): left_blk = left_table[left_idx].astype(jnp.float32)  42.9 us
  transfers between devices with their start and end apart: 5, of which 4 were waited for; matrix products, arithmetic and copies ran while one was open for 9% of the time, Pallas kernels for 0%

profile of v1, /device:TPU:0, one launch (start us, length us, event | category | flops | bytes accessed | tf_op | source)
XLA Modules:
  0.0 748.2 jit_solution(8097626388034483962)
XLA Ops:
  13.0 12.9 %all_gather.7 = bf16[512,256]{1,0:T(8,128)(2,1)S(1)} all-gather(bf16[128,256]{1,0:T(8,128)(2,1)S(1)} %convert_element_type.56), channel_id=1, replica_groups=mesh['grp'=4,'col'=32] {'grp'}, dimensions={0}, use_global_device_ids=true | all-gather | bytes 327680 | tf_op jit(solution)/shard_map/all_gather | solution.py:97
  29.6 7.1 all-gather.2.cloned.1.call-done
  36.7 141.0 %while.26 = (s32[]{:T(128)}, f32[64,8192]{1,0:T(8,128)S(1)}, s32[12,16]{1,0:T(8,128)S(1)}, f32[12,16]{1,0:T(8,128)S(1)}, bf16[12,16,32,1024]{3,2,1,0:T(8,128)(2,...) while((s32[]{:T(128)}, f32[64,8192]{1,0:T(8,128)S(1)}, ...), condition=%wide.region_1.0_spmd.clone, body=%wide.region_0.0_spmd.clone.sunk | while | flops 378802272 | bytes 27796992 | solution.py:80
  39.2 3.9 multiply_convert_fusion.5
  51.0 3.9 multiply_convert_fusion.5
  62.7 3.9 multiply_convert_fusion.5
  74.5 3.9 multiply_convert_fusion.5
  86.3 3.9 multiply_convert_fusion.5
  98.0 3.9 multiply_convert_fusion.5
  179.4 109.9 %all-reduce.9.cloned.1.call-done = (f32[2048,256]{1,0:T(8,128)}, f32[256,256]{0,1:T(8,128)}, f32[256,256]{0,1:T(8,128)}) async-done(((f32[2048,256]{1,0:T(8,128)}, f32[256,256]{0,1:T(8,128)}, f32[256,256]{0,1:T(8,128)}), (f32[2048,256]{1,0:T(8,128)}, f32[256,256]{0,1:T(8,128)}, f32[256,256]{0,1:T(8,128)})) %all-reduce.9.cloned.1.call-update) | async-done | bytes 2621456 | tf_op jit(solution)/shard_map/psum | solution.py:106
  289.5 44.8 %all-reduce.11.cloned.1.call-done = (f32[256,256]{0,1:T(8,128)}, f32[256,256]{0,1:T(8,128)}) async-done(((f32[256,256]{0,1:T(8,128)}, f32[256,256]{0,1:T(8,128)}), (f32[256,256]{0,1:T(8,128)}, f32[256,256]{0,1:T(8,128)})) %all-reduce.11.cloned.1.call-update) | async-done | bytes 524304 | tf_op jit(solution)/shard_map/psum | solution.py:11
  335.6 11.7 %custom-call.29 = f32[128,128]{1,0:T(8,128)S(1)} custom-call(f32[128,128]{1,0:T(8,128)S(1)} %slice.101), custom_call_target="Cholesky" | custom-call | tf_op jit(solution)/shard_map/cholesky/custom-call.2 | solution.py:15
  347.4 9.8 %custom-call.30 = f32[1,128,128]{1,2,0:T(8,128)S(1)} custom-call(f32[1,128,128]{2,1,0:T(8,128)S(1)} %get-tuple-element.265), custom_call_target="InvertDiagBlocksLowerTriangular" | custom-call | tf_op jit(solution)/shard_map/cholesky/custom-call.7 | solution.py:15
  357.9 11.7 %custom-call.31 = f32[128,128]{1,0:T(8,128)S(1)} custom-call(f32[128,128]{1,0:T(8,128)S(1)} %convolution_subtract_fusion.5), custom_call_target="Cholesky" | custom-call | tf_op jit(solution)/shard_map/cholesky/custom-call.3 | solution.py:15
  371.9 4.7 while.24
  376.6 19.7 %custom-call.20 = f32[2,128,128]{1,2,0:T(8,128)S(1)} custom-call(f32[2,128,128]{2,1,0:T(8,128)S(1)} %get-tuple-element.116), custom_call_target="InvertDiagBlocksLowerTriangular" | custom-call | tf_op jit(solution)/shard_map/triangular_solve | solution.py:16
  403.2 4.2 fusion.33
  407.7 42.2 %all-reduce.7.cloned.1.call-done = f32[256,256]{0,1:T(8,128)} async-done(((f32[256,256]{0,1:T(8,128)}), f32[256,256]{0,1:T(8,128)}) %all-reduce.7.cloned.1.call-update) | async-done | bytes 262160 | tf_op jit(solution)/shard_map/psum | solution.py:108
  455.0 216.3 %while.27 = (s32[]{:T(128)}, f32[64,8192]{1,0:T(8,128)S(1)}, s32[12,16]{1,0:T(8,128)}, f32[12,16]{1,0:T(8,128)}, bf16[12,16,32,1024]{3,2,1,0:T(8,128)(2,1)}, /*i...) while((s32[]{:T(128)}, f32[64,8192]{1,0:T(8,128)S(1)}, ...), condition=%wide.region_13.15_spmd.clone, body=%wide.region_12.14_spmd.clone.sunk | while | flops 378802272 | bytes 15213575 | solution.py:80
  460.4 4.4 reshape.345
  464.8 4.3 fusion.116
  478.4 4.4 reshape.345
  482.8 4.3 fusion.116
  496.5 4.4 reshape.345
  500.8 4.3 fusion.116
  514.5 4.4 reshape.345
  518.9 4.3 fusion.116
  532.5 4.4 reshape.345
  536.9 4.3 fusion.116
  550.6 4.4 reshape.345
  554.9 4.3 fusion.116
  568.6 4.4 reshape.345
  572.9 4.3 fusion.116
  586.6 4.4 reshape.345
  591.0 4.3 fusion.116
  604.6 4.4 reshape.345
  609.0 4.3 fusion.116
  622.7 4.4 reshape.345
  627.0 4.3 fusion.116
  640.7 4.4 reshape.345
  645.1 4.3 fusion.116
  658.7 4.4 reshape.345
  663.1 4.3 fusion.116
  675.5 11.7 %custom-call.32 = f32[128,128]{1,0:T(8,128)S(1)} custom-call(f32[128,128]{1,0:T(8,128)S(1)} %slice.104), custom_call_target="Cholesky" | custom-call | tf_op jit(solution)/shard_map/cholesky/custom-call.2 | solution.py:15
  687.3 9.8 %custom-call.33 = f32[1,128,128]{1,2,0:T(8,128)S(1)} custom-call(f32[1,128,128]{2,1,0:T(8,128)S(1)} %get-tuple-element.261), custom_call_target="InvertDiagBlocksLowerTriangular" | custom-call | tf_op jit(solution)/shard_map/cholesky/custom-call.7 | solution.py:15
  697.8 11.7 %custom-call.34 = f32[128,128]{1,0:T(8,128)S(1)} custom-call(f32[128,128]{1,0:T(8,128)S(1)} %convolution_subtract_fusion.4), custom_call_target="Cholesky" | custom-call | tf_op jit(solution)/shard_map/cholesky/custom-call.3 | solution.py:15
  712.1 3.9 while.25
  716.0 19.9 %custom-call.21 = f32[2,128,128]{1,2,0:T(8,128)S(1)} custom-call(f32[2,128,128]{2,1,0:T(8,128)S(1)} %get-tuple-element.124), custom_call_target="InvertDiagBlocksLowerTriangular" | custom-call | tf_op jit(solution)/shard_map/triangular_solve | solution.py:16
  (405 shorter events, 274.0 us)
Async XLA Ops:
  7.2 20.8 %copy-start.5 = (f32[512,256]{1,0:T(8,128)S(1)}, f32[512,256]{1,0:T(8,128)}, u32[]{:S(2)}) copy-start(f32[512,256]{1,0:T(8,128)} %param.17) | copy-start | bytes 1572868
  7.2 29.6 %all-gather.2.cloned.1.call-start = ((), (), s32[]{:S(2)}) async-start(), calls=%async_computation.1 | async-start | bytes 1310720 | tf_op jit(solution)/shard_map/all_gather | solution.py:96
  9.1 280.2 %all-reduce.9.cloned.1.call-start = ((), (), s32[]{:S(2)}) async-start(), calls=%async_computation.4 | async-start | bytes 5242880 | tf_op jit(solution)/shard_map/psum | solution.py:106
  177.8 1.5 copy-start.8
  177.8 1.5 copy-start.9
  179.3 155.0 %all-reduce.11.cloned.1.call-start = ((), (), s32[]{:S(2)}) async-start(), calls=%async_computation.5 | async-start | bytes 1048576 | tf_op jit(solution)/shard_map/psum | solution.py:11
  289.3 160.6 %all-reduce.7.cloned.1.call-start = ((), (), s32[]{:S(2)}) async-start(), calls=%async_computation.2 | async-start | bytes 524288 | tf_op jit(solution)/shard_map/psum | solution.py:108
  335.4 60.9 %copy-start.6 = (f32[2048,256]{1,0:T(8,128)S(1)}, f32[2048,256]{1,0:T(8,128)}, u32[]{:S(2)}) copy-start(f32[2048,256]{1,0:T(8,128)} %get-tuple-element.245) | copy-start | bytes 6291460
  376.6 21.7 %copy-start.10 = (s32[2,2]{1,0:T(2,128)}, s32[2,2]{1,0:T(2,128)S(1)}, u32[]{:S(2)}) copy-start(s32[2,2]{1,0:T(2,128)S(1)} %get-tuple-element.584) | copy-start | bytes 52
  400.2 52.3 %copy-start = (f32[2048,128]{1,0:T(8,128)}, f32[2048,128]{1,0:T(8,128)S(1)}, u32[]{:S(2)}) copy-start(f32[2048,128]{1,0:T(8,128)S(1)} %fusion.48) | copy-start | bytes 3145732
  402.2 1.0 copy-start.2
  407.5 328.5 %reduce-scatter.2.cloned.1.call-start = ((), (), s32[]{:S(2)}) async-start(), calls=%async_computation.3 | async-start | bytes 2621440 | tf_op jit(solution)/shard_map/reduce_scatter | solution.py:117
  672.9 1.2 copy-start.1
  672.9 1.5 copy-start.3
  672.9 2.2 copy-start.4
  672.9 2.2 copy-start.7
  675.3 36.8 %copy-start.11 = (s32[2,2]{1,0:T(2,128)S(1)}, s32[2,2]{1,0:T(2,128)}, u32[]{:S(2)}) copy-start(s32[2,2]{1,0:T(2,128)} %copy-done.10) | copy-start | bytes 52
Sparse Core Ops, SparseCore 0:
  10.2 26.4 all-gather.1
  179.5 109.7 all-reduce.8
  291.7 42.5 all-reduce.10
  407.6 42.2 all-reduce.6
  673.0 30.1 reduce-scatter.1
